TPU v7x, 32 devices: a whole 2x2x4 slice. The times are simulated.
32 devices in a mesh: group: 4 (over x, core), replica: 8 (over z, y).
Axes of the slice: x: 2, y: 2, z: 4, core: 2. Of those that a mesh axis runs over, the one named last changes fastest.
Arguments:
- grad_parts: bfloat16 [8, 8, 128, 512], P('replica', None, 'group'), may hold values from -1 to 1
- owner_order: int32 [8], replicated, may hold values from 0 to 7, each once
- step_count: int32 [1], replicated, may hold values from 1 to 12
- stat_old: float32 [8, 512, 512], P('replica'), as said below
- root_old: bfloat16 [8, 512, 512], P('replica'), may hold values from -0.25 to 0.25
Outputs:
- update: bfloat16 [8, 128, 512], P(None, 'group')
- stat_new: float32 [8, 512, 512], P('replica')
- root_new: bfloat16 [8, 512, 512], P('replica')
Inputs may be any that keep to these rules, and one draw needn't show every extreme that they name: `stat_old`: each matrix is symmetric positive definite.
All inputs are finite; a program needn't handle non-finite values.
Results may differ from a plain program's by a relative error of at most 0.001.
The roundings to bfloat16 on the way count: a program that leaves them out, or rounds other values in their place, can miss the bound.
Values may be sent and summed in bfloat16 or wider, within the bound.
No kernel may reach another device: no remote copies, remote signals or barrier semaphores. Data moves between devices by JAX's collectives and lax.ppermute only.
A program may use at most 64 MiB of HBM per device.

v0:
```python
import functools

import jax
import jax.numpy as jnp
from jax import lax
from jax.experimental import pallas as pl
from jax.experimental.pallas import tpu as pltpu
from jax.sharding import PartitionSpec as P


decay_rate = 0.95
epsilon = 0.001

VMEM = pl.BlockSpec(memory_space=pltpu.VMEM)
SMEM = pl.BlockSpec(memory_space=pltpu.SMEM)
ANY = pl.BlockSpec(memory_space=pl.ANY)
HBM = pl.BlockSpec(memory_space=pltpu.HBM)


def halves(size):
    inner = 2 if size % 2 == 0 else 1
    return size // inner, inner


def is_power(n):
    return n & (n - 1) == 0


def ahead(i, k, n):
    if is_power(n):
        return i ^ k
    return (i + k) % n


def traced_behind(i, k, n):
    return lax.bitwise_xor(i, jnp.int32(k)) if is_power(n) else lax.rem(i + (n - k), n)


def traced_ahead(i, k, n):
    return lax.bitwise_xor(i, jnp.int32(k)) if is_power(n) else lax.rem(i + k, n)


def farthest_first(n):
    return [k for k in range(n - 1, 0, -1)]


def halfway_first(n):
    middle = n // 2
    return [k for k in range(middle, n) if k] + [k for k in range(1, middle)]


def send(x, groups, replicas, dg, dr):
    go, gi = halves(groups)
    ro, ri = halves(replicas)
    pairs = []
    for a in range(go):
        for b in range(gi):
            for c in range(ro):
                for d in range(ri):
                    source = (a * gi + b) * replicas + c * ri + d
                    other_group = ahead(a, dg[0], go) * gi + ahead(b, dg[1], gi)
                    other_replica = ahead(c, dr[0], ro) * ri + ahead(d, dr[1], ri)
                    pairs.append((source, other_group * replicas + other_replica))
    return lax.ppermute(x, ("group", "replica"), pairs)


def pick_kernel(replicas, order_hbm, grads_ref, *rest):
    ro, ri = halves(replicas)
    outs, row_ref = rest[:ro], rest[ro]
    held, order_ref, sem, order_sem = rest[ro + 1 :]
    copy = pltpu.make_async_copy(grads_ref, held, sem)
    copy.start()
    order_copy = pltpu.make_async_copy(order_hbm, order_ref, order_sem)
    order_copy.start()
    me = lax.axis_index("replica")
    outer, inner = lax.div(me, ri), lax.rem(me, ri)
    order_copy.wait()
    positions = lax.broadcasted_iota(jnp.int32, row_ref.shape, 1)
    row = jnp.zeros(row_ref.shape, jnp.int32)
    for slot in range(replicas):
        row = jnp.where(positions == slot, order_ref[slot], row)
    row_ref[...] = row
    copy.wait()
    for k in range(ro):
        for d in range(ri):
            slot = traced_ahead(outer, k, ro) * ri + traced_ahead(inner, d, ri)
            outs[k][d] = held[order_ref[slot]]


def place_kernel(replicas, lots, row_ref, *rest):
    ro, ri = halves(replicas)
    inputs, out_ref, sem = rest[: len(lots)], rest[len(lots)], rest[len(lots) + 1]
    me = lax.axis_index("replica")
    outer, inner = lax.div(me, ri), lax.rem(me, ri)
    row = row_ref[...].astype(jnp.float32)
    positions = lax.broadcasted_iota(jnp.int32, row.shape, 1)
    copies = []
    for ref, offsets in zip(inputs, lots):
        for j, (k, d) in enumerate(offsets):
            slot = traced_behind(outer, k, ro) * ri + traced_behind(inner, d, ri)
            block = jnp.sum(jnp.where(positions == slot, row, 0.0)).astype(jnp.int32)
            copy = pltpu.make_async_copy(ref.at[j], out_ref.at[block], sem.at[len(copies)])
            copy.start()
            copies.append(copy)
    for copy in copies:
        copy.wait()


def graft_kernel(rows, mine_ref, other_ref, root_ref, out_ref):
    mine = mine_ref[...]
    other = other_ref[...]
    root = root_ref[...]
    mine_products = jnp.dot(mine.astype(jnp.bfloat16), root, preferred_element_type=jnp.float32)
    other_products = jnp.dot(other.astype(jnp.bfloat16), root, preferred_element_type=jnp.float32)

    def total(a, b):
        lines = jnp.sum(a * a, axis=0, keepdims=True) + jnp.sum(b * b, axis=0, keepdims=True)
        return jnp.sum(lines, axis=1, keepdims=True)

    graft = jnp.sqrt(total(mine, other) / (total(mine_products, other_products) + 1e-06))
    out_ref[...] = (graft * mine_products[:rows]).astype(jnp.bfloat16)


def dot(a, b):
    return jnp.dot(a, b, preferred_element_type=jnp.float32)


def tiles(n):
    step = 128 if n % 128 == 0 else n
    return [slice(r, r + step) for r in range(0, n, step)]


def square(m_ref, mb_ref, w_ref, wb_ref):
    for r in tiles(m_ref.shape[0]):
        w = 10.0 * m_ref[r] - dot(mb_ref[r], mb_ref[...])
        w_ref[r] = w
        wb_ref[r] = w.astype(jnp.bfloat16)


def quintic(m_ref, mb_ref, w_ref, wb_ref, vb_ref, out_ref, outb_ref):
    n = m_ref.shape[0]
    for r in tiles(n):
        vb_ref[r] = (dot(wb_ref[r], wb_ref[...]) - 50.0 * w_ref[r]).astype(jnp.bfloat16)
    for r in tiles(n):
        m = (625.0 * m_ref[r] + dot(vb_ref[r], mb_ref[...])) * (1.0 / 256.0)
        out_ref[r] = m
        outb_ref[r] = m.astype(jnp.bfloat16)


def eye_rows(r, n):
    rows = lax.broadcasted_iota(jnp.int32, (r.stop - r.start, n), 0) + r.start
    columns = lax.broadcasted_iota(jnp.int32, (r.stop - r.start, n), 1)
    return rows == columns


def stat_kernel(
    corr_ref, mine_ref, other_ref, stat_ref, stat_out, m0, m0b, m1_ref, m1b_ref, c_ref, w, wb, vb
):
    n = stat_ref.shape[0]
    s = jnp.concatenate([mine_ref[...], other_ref[...]], axis=0)
    high = s.astype(jnp.bfloat16)
    low = (s - high.astype(jnp.float32)).astype(jnp.bfloat16)
    left = jnp.concatenate([high, low, high], axis=0)
    right = jnp.concatenate([high, high, low], axis=0)
    corr = corr_ref[0]
    total = jnp.zeros((1, n), jnp.float32)
    for r in tiles(n):
        gram = lax.dot_general(
            left[:, r], right, (((0,), (0,)), ((), ())), preferred_element_type=jnp.float32
        )
        stat = decay_rate * stat_ref[r] + (1.0 - decay_rate) * gram
        stat_out[r] = stat
        shifted = stat * corr + jnp.where(eye_rows(r, n), epsilon, 0.0)
        m0[r] = shifted
        total += jnp.sum(shifted * shifted, axis=0, keepdims=True)
    frobenius = jnp.sqrt(jnp.sum(total, axis=1, keepdims=True))
    inverse = 1.0 / frobenius
    c_ref[...] = jnp.broadcast_to(1.0 / jnp.sqrt(jnp.sqrt(frobenius)), c_ref.shape)
    for r in tiles(n):
        m = m0[r] * inverse
        m0[r] = m
        m0b[r] = m.astype(jnp.bfloat16)
    square(m0, m0b, w, wb)
    quintic(m0, m0b, w, wb, vb, m1_ref, m1b_ref)


def root_kernel(m0, m0b, m1_ref, m1b_ref, c_ref, root_out, w, wb, vb, m2, m2b):
    n = m1_ref.shape[0]
    square(m1_ref, m1b_ref, w, wb)
    quintic(m1_ref, m1b_ref, w, wb, vb, m2, m2b)
    c = c_ref[0:1, 0:1] * (1.0 / 64.0)
    for r in tiles(n):
        h = 5.0 * (m0[r] + m1_ref[r]) - dot(m0b[r], m1b_ref[...])
        x = dot(h.astype(jnp.bfloat16), m2b[...]) - 5.0 * h - 25.0 * m2[r]
        x += jnp.where(eye_rows(r, n), 125.0, 0.0)
        root_out[r] = (c * x).astype(jnp.bfloat16)


def cost(flops, moved):
    return pl.CostEstimate(flops=flops, bytes_accessed=moved, transcendentals=0)


def stay(x):
    return pltpu.with_memory_space_constraint(x, pltpu.HBM)


def grant(moved):
    return pltpu.CompilerParams(vmem_limit_bytes=max(moved, 1 << 20))


def step(groups, replicas, grad_parts, owner_order, step_count, stat_old, root_old):
    go, gi = halves(groups)
    ro, ri = halves(replicas)
    blocks, rows, width = grad_parts.shape[1:]
    hop = functools.partial(send, groups=groups, replicas=replicas)

    pair = jax.ShapeDtypeStruct((ri, rows, width), jnp.bfloat16)
    lanes = 128 * pl.cdiv(replicas, 128)
    *picked, row = pl.pallas_call(
        functools.partial(pick_kernel, replicas),
        out_shape=[pair] * ro + [jax.ShapeDtypeStruct((1, lanes), jnp.int32)],
        in_specs=[HBM, HBM],
        out_specs=[VMEM] * (ro + 1),
        scratch_shapes=[
            pltpu.VMEM((blocks, rows, width), jnp.bfloat16),
            pltpu.SMEM((replicas,), jnp.int32),
            pltpu.SemaphoreType.DMA,
            pltpu.SemaphoreType.DMA,
        ],
        compiler_params=grant(8 * blocks * rows * width),
    )(stay(owner_order), stay(grad_parts[0]))

    partial = picked[0].astype(jnp.float32)
    for k in halfway_first(ro):
        partial = partial + hop(picked[k], dg=(0, 0), dr=(k, 0)).astype(jnp.float32)

    offsets = [(a, d) for a in range(go) for d in range(ri)]
    pieces = {(0, 0): partial[0]}
    for a, d in offsets[1:]:
        pieces[a, d] = hop(partial[d], dg=(a, 0), dr=(0, d))
    lots = [sum((pieces[a, d] for d in range(1, ri)), pieces[a, 0]) for a in range(go)]
    mine = jnp.concatenate(lots, axis=0)
    other = jnp.concatenate([hop(mine, dg=(0, b), dr=(0, 0)) for b in range(1, gi)], axis=0)

    scaled = pl.pallas_call(
        functools.partial(graft_kernel, rows),
        out_shape=jax.ShapeDtypeStruct((rows, width), jnp.bfloat16),
        in_specs=[VMEM] * 3,
        out_specs=VMEM,
        cost_estimate=cost(2 * rows * groups * width * width, 4 * rows * groups * width),
        compiler_params=grant(16 * rows * groups * width + 4 * width * width),
    )(mine, other, root_old[0])

    ks, ds = farthest_first(ro), list(range(1, ri))
    came = []
    for k in ks:
        came.append(hop(scaled, dg=(0, 0), dr=(k, 0)))
    lots = [(scaled[None], [(0, 0)])]
    for d in ds:
        lots.append((hop(scaled, dg=(0, 0), dr=(0, d))[None], [(0, d)]))
    came = jnp.stack(came)
    lots.append((came, [(k, 0) for k in ks]))
    for d in ds:
        lots.append((hop(came, dg=(0, 0), dr=(0, d)), [(k, d) for k in ks]))

    corr = 1.0 / (1.0 - decay_rate ** step_count.astype(jnp.float32))
    full, half = jax.ShapeDtypeStruct((width, width), jnp.float32), jax.ShapeDtypeStruct((width, width), jnp.bfloat16)
    f32, bf16 = pltpu.VMEM(full.shape, full.dtype), pltpu.VMEM(half.shape, half.dtype)
    stat_new, *held = pl.pallas_call(
        stat_kernel,
        out_shape=[full, full, half, full, half, jax.ShapeDtypeStruct((8, 128), jnp.float32)],
        in_specs=[SMEM] + [VMEM] * 3,
        out_specs=[VMEM] * 6,
        scratch_shapes=[f32, bf16, bf16],
        cost_estimate=cost(10 * width**3, 12 * width * width),
        compiler_params=grant(64 * width * width),
    )(corr, mine, other, stat_old[0])
    root_new = pl.pallas_call(
        root_kernel,
        out_shape=half,
        in_specs=[VMEM] * 5,
        out_specs=VMEM,
        scratch_shapes=[f32, bf16, bf16, f32, bf16],
        cost_estimate=cost(6 * width**3, 8 * width * width),
        compiler_params=grant(48 * width * width),
    )(*held)

    update = pl.pallas_call(
        functools.partial(place_kernel, replicas, [offsets for _, offsets in lots]),
        out_shape=jax.ShapeDtypeStruct((blocks, rows, width), jnp.bfloat16),
        in_specs=[VMEM] + [ANY] * len(lots),
        out_specs=ANY,
        scratch_shapes=[pltpu.SemaphoreType.DMA((replicas,))],
        compiler_params=grant(0),
    )(row, *[lot for lot, _ in lots])
    return (update, stat_new[None], root_new[None])


def solution(mesh):
    placed = (
        P("replica", None, "group", None),
        P(),
        P(),
        P("replica", None, None),
        P("replica", None, None),
    )
    return jax.shard_map(
        functools.partial(step, mesh.shape["group"], mesh.shape["replica"]),
        mesh=mesh,
        in_specs=placed,
        out_specs=(P(None, "group", None), P("replica", None, None), P("replica", None, None)),
        check_vma=False,
    )
```

profile of v0, /device:TPU:0, one launch (start us, length us, event | category | flops | bytes accessed | tf_op | source)
XLA Modules:
  0.0 38.1 jit_solution(14656843170705545697)
XLA Ops:
  0.6 1.0 %shard_map.76 = (bf16[2,32,512]{2,1,0:T(8,128)(2,1)S(1)}, bf16[2,32,512]{2,1,0:T(8,128)(2,1)S(1)}, bf16[2,32,512]{2,1,0:T(8,128)(2,1)S(1)}, bf16[2,32,512]{2,1,0:T(8,128)(2,1)S(1)}, s32[1,128]{1,0:T(1,128)S(1)}) custom-call(s32[8]{0:T(128)} %order_hbm.1, bf16[8,32,512]{2,1,0:T(8,128)(2,1)} %bitcast.21), custom_call_target="tpu_custom_call" | custom-call | tf_op jit(solution)/shard_map/pallas_call | solution.py:219
  1.6 4.1 %collective-permute-start = (bf16[2,32,512]{2,1,0:T(8,128)(2,1)S(1)}, bf16[2,32,512]{2,1,0:T(8,128)(2,1)S(1)}, u32[]{:S(2)}, u32[]{:S(2)}) collective-permute-start(bf16[2,32,512]{2,1,0:T(8,128)(2,1)S(1)} %get-tuple-element.16), channel_id=1, source_target_pairs={{0,4},{1,5},{2,6},{3,7},{4,0},{5,1},{6,2},{7,3},{8,12},{9,13},{10,... | collective-permute-start | bytes 196616 | tf_op jit(solution)/shard_map/ppermute | solution.py:64
  5.8 1.3 %collective-permute-start.1 = (bf16[2,32,512]{2,1,0:T(8,128)(2,1)S(1)}, bf16[2,32,512]{2,1,0:T(8,128)(2,1)S(1)}, u32[]{:S(2)}, u32[]{:S(2)}) collective-permute-start(bf16[2,32,512]{2,1,0:T(8,128)(2,1)S(1)} %get-tuple-element.17), channel_id=1, source_target_pairs={{0,6},{1,7},{2,4},{3,5},{4,2},{5,3},{6,0},{7,1},{8,14},{9,15},{10,... | collective-permute-start | bytes 196616 | tf_op jit(solution)/shard_map/ppermute | solution.py:64
  7.1 0.2 collective-permute-start.2
  7.3 2.1 %collective-permute-done = bf16[2,32,512]{2,1,0:T(8,128)(2,1)S(1)} collective-permute-done((bf16[2,32,512]{2,1,0:T(8,128)(2,1)S(1)}, bf16[2,32,512]{2,1,0:T(8,128)(2,1)S(1)}, u32[]{:S(2)}, u32[]{:S(2)}) %collective-permute-start) | collective-permute-done | bytes 65568 | tf_op jit(solution)/shard_map/ppermute | solution.py:64
  9.5 2.5 %collective-permute-done.1 = bf16[2,32,512]{2,1,0:T(8,128)(2,1)S(1)} collective-permute-done((bf16[2,32,512]{2,1,0:T(8,128)(2,1)S(1)}, bf16[2,32,512]{2,1,0:T(8,128)(2,1)S(1)}, u32[]{:S(2)}, u32[]{:S(2)}) %collective-permute-start.1) | collective-permute-done | bytes 65568 | tf_op jit(solution)/shard_map/ppermute | solution.py:64
  11.9 0.1 collective-permute-done.2
  12.2 1.6 %collective-permute-start.3 = (f32[32,512]{1,0:T(8,128)S(1)}, f32[32,512]{1,0:T(8,128)S(1)}, u32[]{:S(2)}, u32[]{:S(2)}) collective-permute-start(f32[32,512]{1,0:T(8,128)S(1)} %get-tuple-element.25), channel_id=1, source_target_pairs={{0,1},{1,0},{2,3},{3,2},{4,5},{5,4},{6,7},{7,6},{8,9},{9,8},{10,11... | collective-permute-start | bytes 196616 | tf_op jit(solution)/shard_map/ppermute | solution.py:64
  13.7 1.4 %collective-permute-start.5 = (f32[32,512]{1,0:T(8,128)S(1)}, f32[32,512]{1,0:T(8,128)S(1)}, u32[]{:S(2)}, u32[]{:S(2)}) collective-permute-start(f32[32,512]{1,0:T(8,128)S(1)} %get-tuple-element.25), channel_id=1, source_target_pairs={{0,17},{1,16},{2,19},{3,18},{4,21},{5,20},{6,23},{7,22},{8,25},{9,... | collective-permute-start | bytes 196616 | tf_op jit(solution)/shard_map/ppermute | solution.py:64
  15.2 0.5 %collective-permute-start.4 = (f32[32,512]{1,0:T(8,128)S(1)}, f32[32,512]{1,0:T(8,128)S(1)}, u32[]{:S(2)}, u32[]{:S(2)}) collective-permute-start(f32[32,512]{1,0:T(8,128)S(1)} %get-tuple-element.26), channel_id=1, source_target_pairs={{0,16},{1,17},{2,18},{3,19},{4,20},{5,21},{6,22},{7,23},{8,24},{9,... | collective-permute-start | bytes 196616 | tf_op jit(solution)/shard_map/ppermute | solution.py:64
  15.7 1.3 %collective-permute-done.3 = f32[32,512]{1,0:T(8,128)S(1)} collective-permute-done((f32[32,512]{1,0:T(8,128)S(1)}, f32[32,512]{1,0:T(8,128)S(1)}, u32[]{:S(2)}, u32[]{:S(2)}) %collective-permute-start.3) | collective-permute-done | bytes 65568 | tf_op jit(solution)/shard_map/ppermute | solution.py:64
  17.0 2.4 %collective-permute-done.4 = f32[32,512]{1,0:T(8,128)S(1)} collective-permute-done((f32[32,512]{1,0:T(8,128)S(1)}, f32[32,512]{1,0:T(8,128)S(1)}, u32[]{:S(2)}, u32[]{:S(2)}) %collective-permute-start.4) | collective-permute-done | bytes 65568 | tf_op jit(solution)/shard_map/ppermute | solution.py:64
  19.5 0.1 collective-permute-start.6
  19.6 1.3 %collective-permute-done.6.other_ref = f32[64,512]{1,0:T(8,128)S(1)} collective-permute-done((f32[64,512]{1,0:T(8,128)S(1)}, f32[64,512]{1,0:T(8,128)S(1)}, u32[]{:S(2)}, u32[]{:S(2)}) %collective-permute-start.6) | collective-permute-done | bytes 131104 | tf_op jit(solution)/shard_map/ppermute | solution.py:64
  20.9 0.4 %shard_map.77 = bf16[32,512]{1,0:T(8,128)(2,1)S(1)} custom-call(f32[64,512]{1,0:T(8,128)S(1)} %pad_maximum_fusion.mine_ref, f32[64,512]{1,0:T(8,128)S(1)} %collective-permute-done.6.other_ref, bf16[512,512]{1,0:T(8,128)(2,1)S(1)} %bitcast.16), custom_call_target="tpu_custom_call" | custom-call | flops 67108864 | bytes 262144 | tf_op jit(solution)/shard_map/pallas_call | solution.py:245
  21.3 1.0 %collective-permute-start.10 = (bf16[32,512]{1,0:T(8,128)(2,1)S(1)}, bf16[32,512]{1,0:T(8,128)(2,1)S(1)}, u32[]{:S(2)}, u32[]{:S(2)}) collective-permute-start(bf16[32,512]{1,0:T(8,128)(2,1)S(1)} %shard_map.77), channel_id=1, source_target_pairs={{0,2},{1,3},{2,0},{3,1},{4,6},{5,7},{6,4},{7,5},{8,10},{9,11},{10,... | collective-permute-start | bytes 98312 | tf_op jit(solution)/shard_map/ppermute | solution.py:64
  22.3 2.6 %collective-permute-start.9 = (bf16[32,512]{1,0:T(8,128)(2,1)S(1)}, bf16[32,512]{1,0:T(8,128)(2,1)S(1)}, u32[]{:S(2)}, u32[]{:S(2)}) collective-permute-start(bf16[32,512]{1,0:T(8,128)(2,1)S(1)} %shard_map.77), channel_id=1, source_target_pairs={{0,4},{1,5},{2,6},{3,7},{4,0},{5,1},{6,2},{7,3},{8,12},{9,13},{10,... | collective-permute-start | bytes 98312 | tf_op jit(solution)/shard_map/ppermute | solution.py:64
  24.9 0.8 %collective-permute-start.8 = (bf16[32,512]{1,0:T(8,128)(2,1)S(1)}, bf16[32,512]{1,0:T(8,128)(2,1)S(1)}, u32[]{:S(2)}, u32[]{:S(2)}) collective-permute-start(bf16[32,512]{1,0:T(8,128)(2,1)S(1)} %shard_map.77), channel_id=1, source_target_pairs={{0,6},{1,7},{2,4},{3,5},{4,2},{5,3},{6,0},{7,1},{8,14},{9,15},{10,... | collective-permute-start | bytes 98312 | tf_op jit(solution)/shard_map/ppermute | solution.py:64
  26.5 1.6 %collective-permute-start.7 = (bf16[32,512]{1,0:T(8,128)(2,1)S(1)}, bf16[32,512]{1,0:T(8,128)(2,1)S(1)}, u32[]{:S(2)}, u32[]{:S(2)}) collective-permute-start(bf16[32,512]{1,0:T(8,128)(2,1)S(1)} %shard_map.77), channel_id=1, source_target_pairs={{0,1},{1,0},{2,3},{3,2},{4,5},{5,4},{6,7},{7,6},{8,9},{9,8},{10,11... | collective-permute-start | bytes 98312 | tf_op jit(solution)/shard_map/ppermute | solution.py:64
  28.1 2.6 %collective-permute-done.8 = bf16[32,512]{1,0:T(8,128)(2,1)S(1)} collective-permute-done((bf16[32,512]{1,0:T(8,128)(2,1)S(1)}, bf16[32,512]{1,0:T(8,128)(2,1)S(1)}, u32[]{:S(2)}, u32[]{:S(2)}) %collective-permute-start.8) | collective-permute-done | bytes 32800 | tf_op jit(solution)/shard_map/ppermute | solution.py:64
  30.7 1.6 %collective-permute-start.11 = (bf16[3,32,512]{2,1,0:T(8,128)(2,1)S(1)}, bf16[3,32,512]{2,1,0:T(8,128)(2,1)S(1)}, u32[]{:S(2)}, u32[]{:S(2)}) collective-permute-start(bf16[3,32,512]{2,1,0:T(8,128)(2,1)S(1)} %pad_maximum_fusion.1.rest_2_), channel_id=1, source_target_pairs={{0,1},{1,0},{2,3},{3,2},{4,5},{5,4},{6,7},{7,6},{8,9},{9,8},{10,11... | collective-permute-start | bytes 294920 | tf_op jit(solution)/shard_map/ppermute | solution.py:64
  32.2 2.0 %shard_map.79 = (f32[512,512]{1,0:T(8,128)}, f32[512,512]{1,0:T(8,128)S(1)}, bf16[512,512]{1,0:T(8,128)(2,1)S(1)}, f32[512,512]{1,0:T(8,128)S(1)}, bf16[512,512]{1,0:T(8,128)(2,1)S(1)}, /*index=5*/f32[8,128]{1,0:T(8,128)S(1)}) custom-call(f32[1]{0:T(128)S(6)} %div.3.corr_ref, f32[64,512]{1,0:T(8,128)S(1)} %pad_maximum_fusion.mine_ref, ...), custom_call_target="tpu_custom_call" | custom-call | flops 1342177280 | bytes 3145728 | tf_op jit(solution)/shard_map/pallas_call | solution.py:269
  34.3 3.0 %shard_map.80 = bf16[512,512]{1,0:T(8,128)(2,1)} custom-call(f32[512,512]{1,0:T(8,128)S(1)} %get-tuple-element.20.m0, bf16[512,512]{1,0:T(8,128)(2,1)S(1)} %get-tuple-element.21.m0b, f32[512,512]{1,0:T(8,128)S(1)} %get-tuple-element.22.m1_ref, bf16[512,512]{1,0:T(8,128)(2,1)S(1)} %get-tuple-element.23.m1b_ref, f32[8,128]{1,0:T(8,128)S(1)} %get-tuple-element.24.c_ref), custom_call_target="tpu_custom_call" | custom-call | flops 805306368 | bytes 2097152 | tf_op jit(solution)/shard_map/pallas_call | solution.py:278
  37.3 0.9 %shard_map.78 = bf16[8,32,512]{2,1,0:T(8,128)(2,1)} custom-call(s32[1,128]{1,0:T(1,128)S(1)} %get-tuple-element.14.row_ref, bf16[1,32,512]{2,1,0:T(8,128)(2,1)S(1)} %bitcast.17, bf16[1,32,512]{2,1,0:T(8,128)(2,1)S(1)} %bitcast.18, bf16[3,32,512]{2,1,0:T(8,128)(2,1)S(1)} %pad_maximum_fusion.1.rest_2_, bf16[3,32,512]{2,1,0:T(8,128)(2,1)S(1)} %collective-permute-done.11.rest_3_), custom_call_target="tpu_custom_call" | custom-call | tf_op jit(solution)/shard_map/pallas_call | solution.py:288
  (15 shorter events, 0.1 us)
Async XLA Ops:
  1.6 7.8 %collective-permute-start = (bf16[2,32,512]{2,1,0:T(8,128)(2,1)S(1)}, bf16[2,32,512]{2,1,0:T(8,128)(2,1)S(1)}, u32[]{:S(2)}, u32[]{:S(2)}) collective-permute-start(bf16[2,32,512]{2,1,0:T(8,128)(2,1)S(1)} %get-tuple-element.16), channel_id=1, source_target_pairs={{0,4},{1,5},{2,6},{3,7},{4,0},{5,1},{6,2},{7,3},{8,12},{9,13},{10,... | collective-permute-start | bytes 196616 | tf_op jit(solution)/shard_map/ppermute | solution.py:64
  5.8 6.2 %collective-permute-start.1 = (bf16[2,32,512]{2,1,0:T(8,128)(2,1)S(1)}, bf16[2,32,512]{2,1,0:T(8,128)(2,1)S(1)}, u32[]{:S(2)}, u32[]{:S(2)}) collective-permute-start(bf16[2,32,512]{2,1,0:T(8,128)(2,1)S(1)} %get-tuple-element.17), channel_id=1, source_target_pairs={{0,6},{1,7},{2,4},{3,5},{4,2},{5,3},{6,0},{7,1},{8,14},{9,15},{10,... | collective-permute-start | bytes 196616 | tf_op jit(solution)/shard_map/ppermute | solution.py:64
  7.1 5.0 %collective-permute-start.2 = (bf16[2,32,512]{2,1,0:T(8,128)(2,1)S(1)}, bf16[2,32,512]{2,1,0:T(8,128)(2,1)S(1)}, u32[]{:S(2)}, u32[]{:S(2)}) collective-permute-start(bf16[2,32,512]{2,1,0:T(8,128)(2,1)S(1)} %get-tuple-element.18), channel_id=1, source_target_pairs={{0,2},{1,3},{2,0},{3,1},{4,6},{5,7},{6,4},{7,5},{8,10},{9,11},{10,... | collective-permute-start | bytes 196616 | tf_op jit(solution)/shard_map/ppermute | solution.py:64
  12.1 8.8 %copy-start = (bf16[1,512,512]{2,1,0:T(8,128)(2,1)S(1)}, bf16[1,512,512]{2,1,0:T(8,128)(2,1)}, u32[]{:S(2)}) copy-start(bf16[1,512,512]{2,1,0:T(8,128)(2,1)} %param.9) | copy-start | bytes 1572868
  12.1 20.1 %copy-start.1 = (f32[1,512,512]{2,1,0:T(8,128)S(1)}, f32[1,512,512]{2,1,0:T(8,128)}, u32[]{:S(2)}) copy-start(f32[1,512,512]{2,1,0:T(8,128)} %param.8) | copy-start | bytes 3145732
  12.2 4.8 %collective-permute-start.3 = (f32[32,512]{1,0:T(8,128)S(1)}, f32[32,512]{1,0:T(8,128)S(1)}, u32[]{:S(2)}, u32[]{:S(2)}) collective-permute-start(f32[32,512]{1,0:T(8,128)S(1)} %get-tuple-element.25), channel_id=1, source_target_pairs={{0,1},{1,0},{2,3},{3,2},{4,5},{5,4},{6,7},{7,6},{8,9},{9,8},{10,11... | collective-permute-start | bytes 196616 | tf_op jit(solution)/shard_map/ppermute | solution.py:64
  13.7 5.7 %collective-permute-start.5 = (f32[32,512]{1,0:T(8,128)S(1)}, f32[32,512]{1,0:T(8,128)S(1)}, u32[]{:S(2)}, u32[]{:S(2)}) collective-permute-start(f32[32,512]{1,0:T(8,128)S(1)} %get-tuple-element.25), channel_id=1, source_target_pairs={{0,17},{1,16},{2,19},{3,18},{4,21},{5,20},{6,23},{7,22},{8,25},{9,... | collective-permute-start | bytes 196616 | tf_op jit(solution)/shard_map/ppermute | solution.py:64
  15.2 4.3 %collective-permute-start.4 = (f32[32,512]{1,0:T(8,128)S(1)}, f32[32,512]{1,0:T(8,128)S(1)}, u32[]{:S(2)}, u32[]{:S(2)}) collective-permute-start(f32[32,512]{1,0:T(8,128)S(1)} %get-tuple-element.26), channel_id=1, source_target_pairs={{0,16},{1,17},{2,18},{3,19},{4,20},{5,21},{6,22},{7,23},{8,24},{9,... | collective-permute-start | bytes 196616 | tf_op jit(solution)/shard_map/ppermute | solution.py:64
  19.5 1.4 %collective-permute-start.6 = (f32[64,512]{1,0:T(8,128)S(1)}, f32[64,512]{1,0:T(8,128)S(1)}, u32[]{:S(2)}, u32[]{:S(2)}) collective-permute-start(f32[64,512]{1,0:T(8,128)S(1)} %pad_maximum_fusion.mine_ref), channel_id=1, source_target_pairs={{0,8},{1,9},{2,10},{3,11},{4,12},{5,13},{6,14},{7,15},{8,0},{9,1},... | collective-permute-start | bytes 393224 | tf_op jit(solution)/shard_map/ppermute | solution.py:64
  21.3 6.8 %collective-permute-start.10 = (bf16[32,512]{1,0:T(8,128)(2,1)S(1)}, bf16[32,512]{1,0:T(8,128)(2,1)S(1)}, u32[]{:S(2)}, u32[]{:S(2)}) collective-permute-start(bf16[32,512]{1,0:T(8,128)(2,1)S(1)} %shard_map.77), channel_id=1, source_target_pairs={{0,2},{1,3},{2,0},{3,1},{4,6},{5,7},{6,4},{7,5},{8,10},{9,11},{10,... | collective-permute-start | bytes 98312 | tf_op jit(solution)/shard_map/ppermute | solution.py:64
  22.3 5.8 %collective-permute-start.9 = (bf16[32,512]{1,0:T(8,128)(2,1)S(1)}, bf16[32,512]{1,0:T(8,128)(2,1)S(1)}, u32[]{:S(2)}, u32[]{:S(2)}) collective-permute-start(bf16[32,512]{1,0:T(8,128)(2,1)S(1)} %shard_map.77), channel_id=1, source_target_pairs={{0,4},{1,5},{2,6},{3,7},{4,0},{5,1},{6,2},{7,3},{8,12},{9,13},{10,... | collective-permute-start | bytes 98312 | tf_op jit(solution)/shard_map/ppermute | solution.py:64
  24.9 5.7 %collective-permute-start.8 = (bf16[32,512]{1,0:T(8,128)(2,1)S(1)}, bf16[32,512]{1,0:T(8,128)(2,1)S(1)}, u32[]{:S(2)}, u32[]{:S(2)}) collective-permute-start(bf16[32,512]{1,0:T(8,128)(2,1)S(1)} %shard_map.77), channel_id=1, source_target_pairs={{0,6},{1,7},{2,4},{3,5},{4,2},{5,3},{6,0},{7,1},{8,14},{9,15},{10,... | collective-permute-start | bytes 98312 | tf_op jit(solution)/shard_map/ppermute | solution.py:64
  26.5 10.8 %collective-permute-start.7 = (bf16[32,512]{1,0:T(8,128)(2,1)S(1)}, bf16[32,512]{1,0:T(8,128)(2,1)S(1)}, u32[]{:S(2)}, u32[]{:S(2)}) collective-permute-start(bf16[32,512]{1,0:T(8,128)(2,1)S(1)} %shard_map.77), channel_id=1, source_target_pairs={{0,1},{1,0},{2,3},{3,2},{4,5},{5,4},{6,7},{7,6},{8,9},{9,8},{10,11... | collective-permute-start | bytes 98312 | tf_op jit(solution)/shard_map/ppermute | solution.py:64
  30.7 6.6 %collective-permute-start.11 = (bf16[3,32,512]{2,1,0:T(8,128)(2,1)S(1)}, bf16[3,32,512]{2,1,0:T(8,128)(2,1)S(1)}, u32[]{:S(2)}, u32[]{:S(2)}) collective-permute-start(bf16[3,32,512]{2,1,0:T(8,128)(2,1)S(1)} %pad_maximum_fusion.1.rest_2_), channel_id=1, source_target_pairs={{0,1},{1,0},{2,3},{3,2},{4,5},{5,4},{6,7},{7,6},{8,9},{9,8},{10,11... | collective-permute-start | bytes 294920 | tf_op jit(solution)/shard_map/ppermute | solution.py:64
where the time goes:
time: 38.3 us; the launch traced here: 38.1 us
  starting transfers between devices  17 us (44%)
  waiting for transfers between devices  12.4 us (32%)
  Pallas kernels  7.28 us (19%)
  between operations  1.45 us (4%)
    ppermute x12, starting transfers between devices, send(): return lax.ppermute(x, ('group', 'replica'), pairs)  17 us
    ppermute x12, waiting for transfers between devices, send(): return lax.ppermute(x, ('group', 'replica'), pairs)  12.4 us
    pallas_call x1, Pallas kernels, step(): pl.pallas_call(root_kernel, out_shape=half, in_specs=[VMEM] * 5, out_spec...  3 us
    pallas_call x1, Pallas kernels, step(): pl.pallas_call(stat_kernel, out_shape=[full, full, half, full, half, jax....  2.01 us
    pallas_call x1, Pallas kernels, step(): pl.pallas_call(functools.partial(pick_kernel, replicas), out_shape=[pair]...  0.99 us
    pallas_call x1, Pallas kernels, step(): pl.pallas_call(functools.partial(place_kernel, replicas, [offsets for _,...  0.88 us
  transfers between devices with their start and end apart: 12, of which 7 were waited for; matrix products, arithmetic and copies ran while one was open for 0% of the time, Pallas kernels for 13%

commit v1 on v0

--- a/solution.py
+++ b/solution.py
@@ -106,19 +106,26 @@
         copy.wait()
 
 
-def graft_kernel(rows, mine_ref, other_ref, root_ref, out_ref):
+def product_kernel(rows, mine_ref, root_ref, product_ref, norm_ref):
     mine = mine_ref[...]
+    products = dot(mine.astype(jnp.bfloat16), root_ref[...])
+    product_ref[...] = products[:rows]
+    for row, x in enumerate((mine, products)):
+        total = jnp.sum(jnp.sum(x * x, axis=0, keepdims=True), axis=1, keepdims=True)
+        norm_ref[row : row + 1] = jnp.broadcast_to(total, (1, norm_ref.shape[1]))
+
+
+def graft_kernel(other_ref, root_ref, product_ref, norm_ref, out_ref):
     other = other_ref[...]
-    root = root_ref[...]
-    mine_products = jnp.dot(mine.astype(jnp.bfloat16), root, preferred_element_type=jnp.float32)
-    other_products = jnp.dot(other.astype(jnp.bfloat16), root, preferred_element_type=jnp.float32)
-
-    def total(a, b):
-        lines = jnp.sum(a * a, axis=0, keepdims=True) + jnp.sum(b * b, axis=0, keepdims=True)
-        return jnp.sum(lines, axis=1, keepdims=True)
-
-    graft = jnp.sqrt(total(mine, other) / (total(mine_products, other_products) + 1e-06))
-    out_ref[...] = (graft * mine_products[:rows]).astype(jnp.bfloat16)
+    others = dot(other.astype(jnp.bfloat16), root_ref[...])
+
+    def total(x):
+        return jnp.sum(jnp.sum(x * x, axis=0, keepdims=True), axis=1, keepdims=True)
+
+    grad_norm = norm_ref[0:1, 0:1] + total(other)
+    update_norm = norm_ref[1:2, 0:1] + total(others)
+    graft = jnp.sqrt(grad_norm / (update_norm + 1e-06))
+    out_ref[...] = (graft * product_ref[...]).astype(jnp.bfloat16)
 
 
 def dot(a, b):
@@ -240,16 +247,27 @@
         pieces[a, d] = hop(partial[d], dg=(a, 0), dr=(0, d))
     lots = [sum((pieces[a, d] for d in range(1, ri)), pieces[a, 0]) for a in range(go)]
     mine = jnp.concatenate(lots, axis=0)
-    other = jnp.concatenate([hop(mine, dg=(0, b), dr=(0, 0)) for b in range(1, gi)], axis=0)
-
+    others = []
+    for b in range(1, gi):
+        others.append(hop(mine, dg=(0, b), dr=(0, 0)))
+    other = jnp.concatenate(others, axis=0)
+
+    products, norms = pl.pallas_call(
+        functools.partial(product_kernel, rows),
+        out_shape=[jax.ShapeDtypeStruct((rows, width), jnp.float32), jax.ShapeDtypeStruct((2, 128), jnp.float32)],
+        in_specs=[VMEM] * 2,
+        out_specs=[VMEM] * 2,
+        cost_estimate=cost(2 * rows * go * width * width, 4 * rows * go * width),
+        compiler_params=grant(16 * rows * groups * width + 4 * width * width),
+    )(mine, root_old[0])
     scaled = pl.pallas_call(
-        functools.partial(graft_kernel, rows),
+        graft_kernel,
         out_shape=jax.ShapeDtypeStruct((rows, width), jnp.bfloat16),
-        in_specs=[VMEM] * 3,
+        in_specs=[VMEM] * 4,
         out_specs=VMEM,
         cost_estimate=cost(2 * rows * groups * width * width, 4 * rows * groups * width),
         compiler_params=grant(16 * rows * groups * width + 4 * width * width),
-    )(mine, other, root_old[0])
+    )(other, root_old[0], products, norms)
 
     ks, ds = farthest_first(ro), list(range(1, ri))
     came = []

time: 38.3 us -> 38.2 us (level)
  waiting for transfers between devices: 12.4 us -> 12 us
  transfers between devices with their start and end apart: 12 -> 12, of which waited for: 7 -> 7; matrix products, arithmetic and copies ran while one was open for 0% -> 0% of each run, Pallas kernels for 13% -> 14%
where the time goes in v1:
time: 38.2 us; the launch traced here: 38.1 us
  starting transfers between devices  17 us (45%)
  waiting for transfers between devices  12 us (31%)
  Pallas kernels  7.51 us (20%)
  between operations  1.46 us (4%)
    ppermute x12, starting transfers between devices, send(): return lax.ppermute(x, ('group', 'replica'), pairs)  17 us
    ppermute x12, waiting for transfers between devices, send(): return lax.ppermute(x, ('group', 'replica'), pairs)  12 us
    pallas_call x1, Pallas kernels, step(): pl.pallas_call(root_kernel, out_shape=half, in_specs=[VMEM] * 5, out_spec...  3 us
    pallas_call x1, Pallas kernels, step(): pl.pallas_call(stat_kernel, out_shape=[full, full, half, full, half, jax....  2 us
    pallas_call x1, Pallas kernels, step(): pl.pallas_call(functools.partial(pick_kernel, replicas), out_shape=[pair]...  0.99 us
    pallas_call x1, Pallas kernels, step(): pl.pallas_call(functools.partial(place_kernel, replicas, [offsets for _,...  0.88 us
  transfers between devices with their start and end apart: 12, of which 7 were waited for; matrix products, arithmetic and copies ran while one was open for 0% of the time, Pallas kernels for 14%

profile of v1, /device:TPU:0, one launch (start us, length us, event | category | flops | bytes accessed | tf_op | source)
XLA Modules:
  0.0 38.1 jit_solution(16962762981896634395)
XLA Ops:
  0.6 1.0 %shard_map.76 = (bf16[2,32,512]{2,1,0:T(8,128)(2,1)S(1)}, bf16[2,32,512]{2,1,0:T(8,128)(2,1)S(1)}, bf16[2,32,512]{2,1,0:T(8,128)(2,1)S(1)}, bf16[2,32,512]{2,1,0:T(8,128)(2,1)S(1)}, s32[1,128]{1,0:T(1,128)S(1)}) custom-call(s32[8]{0:T(128)} %order_hbm.1, bf16[8,32,512]{2,1,0:T(8,128)(2,1)} %bitcast.22), custom_call_target="tpu_custom_call" | custom-call | tf_op jit(solution)/shard_map/pallas_call | solution.py:226
  1.6 4.1 %collective-permute-start = (bf16[2,32,512]{2,1,0:T(8,128)(2,1)S(1)}, bf16[2,32,512]{2,1,0:T(8,128)(2,1)S(1)}, u32[]{:S(2)}, u32[]{:S(2)}) collective-permute-start(bf16[2,32,512]{2,1,0:T(8,128)(2,1)S(1)} %get-tuple-element.18), channel_id=1, source_target_pairs={{0,4},{1,5},{2,6},{3,7},{4,0},{5,1},{6,2},{7,3},{8,12},{9,13},{10,... | collective-permute-start | bytes 196616 | tf_op jit(solution)/shard_map/ppermute | solution.py:64
  5.8 1.3 %collective-permute-start.1 = (bf16[2,32,512]{2,1,0:T(8,128)(2,1)S(1)}, bf16[2,32,512]{2,1,0:T(8,128)(2,1)S(1)}, u32[]{:S(2)}, u32[]{:S(2)}) collective-permute-start(bf16[2,32,512]{2,1,0:T(8,128)(2,1)S(1)} %get-tuple-element.19), channel_id=1, source_target_pairs={{0,6},{1,7},{2,4},{3,5},{4,2},{5,3},{6,0},{7,1},{8,14},{9,15},{10,... | collective-permute-start | bytes 196616 | tf_op jit(solution)/shard_map/ppermute | solution.py:64
  7.1 0.2 collective-permute-start.2
  7.3 2.1 %collective-permute-done = bf16[2,32,512]{2,1,0:T(8,128)(2,1)S(1)} collective-permute-done((bf16[2,32,512]{2,1,0:T(8,128)(2,1)S(1)}, bf16[2,32,512]{2,1,0:T(8,128)(2,1)S(1)}, u32[]{:S(2)}, u32[]{:S(2)}) %collective-permute-start) | collective-permute-done | bytes 65568 | tf_op jit(solution)/shard_map/ppermute | solution.py:64
  9.5 2.5 %collective-permute-done.1 = bf16[2,32,512]{2,1,0:T(8,128)(2,1)S(1)} collective-permute-done((bf16[2,32,512]{2,1,0:T(8,128)(2,1)S(1)}, bf16[2,32,512]{2,1,0:T(8,128)(2,1)S(1)}, u32[]{:S(2)}, u32[]{:S(2)}) %collective-permute-start.1) | collective-permute-done | bytes 65568 | tf_op jit(solution)/shard_map/ppermute | solution.py:64
  11.9 0.1 collective-permute-done.2
  12.1 1.6 %collective-permute-start.3 = (f32[32,512]{1,0:T(8,128)S(1)}, f32[32,512]{1,0:T(8,128)S(1)}, u32[]{:S(2)}, u32[]{:S(2)}) collective-permute-start(f32[32,512]{1,0:T(8,128)S(1)} %get-tuple-element.29), channel_id=1, source_target_pairs={{0,1},{1,0},{2,3},{3,2},{4,5},{5,4},{6,7},{7,6},{8,9},{9,8},{10,11... | collective-permute-start | bytes 196616 | tf_op jit(solution)/shard_map/ppermute | solution.py:64
  13.7 1.4 %collective-permute-start.5 = (f32[32,512]{1,0:T(8,128)S(1)}, f32[32,512]{1,0:T(8,128)S(1)}, u32[]{:S(2)}, u32[]{:S(2)}) collective-permute-start(f32[32,512]{1,0:T(8,128)S(1)} %get-tuple-element.29), channel_id=1, source_target_pairs={{0,17},{1,16},{2,19},{3,18},{4,21},{5,20},{6,23},{7,22},{8,25},{9,... | collective-permute-start | bytes 196616 | tf_op jit(solution)/shard_map/ppermute | solution.py:64
  15.2 0.5 %collective-permute-start.4 = (f32[32,512]{1,0:T(8,128)S(1)}, f32[32,512]{1,0:T(8,128)S(1)}, u32[]{:S(2)}, u32[]{:S(2)}) collective-permute-start(f32[32,512]{1,0:T(8,128)S(1)} %get-tuple-element.30), channel_id=1, source_target_pairs={{0,16},{1,17},{2,18},{3,19},{4,20},{5,21},{6,22},{7,23},{8,24},{9,... | collective-permute-start | bytes 196616 | tf_op jit(solution)/shard_map/ppermute | solution.py:64
  15.7 1.3 %collective-permute-done.3 = f32[32,512]{1,0:T(8,128)S(1)} collective-permute-done((f32[32,512]{1,0:T(8,128)S(1)}, f32[32,512]{1,0:T(8,128)S(1)}, u32[]{:S(2)}, u32[]{:S(2)}) %collective-permute-start.3) | collective-permute-done | bytes 65568 | tf_op jit(solution)/shard_map/ppermute | solution.py:64
  17.0 2.4 %collective-permute-done.4 = f32[32,512]{1,0:T(8,128)S(1)} collective-permute-done((f32[32,512]{1,0:T(8,128)S(1)}, f32[32,512]{1,0:T(8,128)S(1)}, u32[]{:S(2)}, u32[]{:S(2)}) %collective-permute-start.4) | collective-permute-done | bytes 65568 | tf_op jit(solution)/shard_map/ppermute | solution.py:64
  19.6 0.3 shard_map.77
  19.8 1.0 %collective-permute-done.6.other_ref = f32[64,512]{1,0:T(8,128)S(1)} collective-permute-done((f32[64,512]{1,0:T(8,128)S(1)}, f32[64,512]{1,0:T(8,128)S(1)}, u32[]{:S(2)}, u32[]{:S(2)}) %collective-permute-start.6) | collective-permute-done | bytes 131104 | tf_op jit(solution)/shard_map/ppermute | solution.py:64
  20.9 0.4 shard_map.78
  21.2 1.0 %collective-permute-start.10 = (bf16[32,512]{1,0:T(8,128)(2,1)S(1)}, bf16[32,512]{1,0:T(8,128)(2,1)S(1)}, u32[]{:S(2)}, u32[]{:S(2)}) collective-permute-start(bf16[32,512]{1,0:T(8,128)(2,1)S(1)} %shard_map.78), channel_id=1, source_target_pairs={{0,2},{1,3},{2,0},{3,1},{4,6},{5,7},{6,4},{7,5},{8,10},{9,11},{10,... | collective-permute-start | bytes 98312 | tf_op jit(solution)/shard_map/ppermute | solution.py:64
  22.2 2.6 %collective-permute-start.9 = (bf16[32,512]{1,0:T(8,128)(2,1)S(1)}, bf16[32,512]{1,0:T(8,128)(2,1)S(1)}, u32[]{:S(2)}, u32[]{:S(2)}) collective-permute-start(bf16[32,512]{1,0:T(8,128)(2,1)S(1)} %shard_map.78), channel_id=1, source_target_pairs={{0,4},{1,5},{2,6},{3,7},{4,0},{5,1},{6,2},{7,3},{8,12},{9,13},{10,... | collective-permute-start | bytes 98312 | tf_op jit(solution)/shard_map/ppermute | solution.py:64
  24.9 0.8 %collective-permute-start.8 = (bf16[32,512]{1,0:T(8,128)(2,1)S(1)}, bf16[32,512]{1,0:T(8,128)(2,1)S(1)}, u32[]{:S(2)}, u32[]{:S(2)}) collective-permute-start(bf16[32,512]{1,0:T(8,128)(2,1)S(1)} %shard_map.78), channel_id=1, source_target_pairs={{0,6},{1,7},{2,4},{3,5},{4,2},{5,3},{6,0},{7,1},{8,14},{9,15},{10,... | collective-permute-start | bytes 98312 | tf_op jit(solution)/shard_map/ppermute | solution.py:64
  26.4 1.6 %collective-permute-start.7 = (bf16[32,512]{1,0:T(8,128)(2,1)S(1)}, bf16[32,512]{1,0:T(8,128)(2,1)S(1)}, u32[]{:S(2)}, u32[]{:S(2)}) collective-permute-start(bf16[32,512]{1,0:T(8,128)(2,1)S(1)} %shard_map.78), channel_id=1, source_target_pairs={{0,1},{1,0},{2,3},{3,2},{4,5},{5,4},{6,7},{7,6},{8,9},{9,8},{10,11... | collective-permute-start | bytes 98312 | tf_op jit(solution)/shard_map/ppermute | solution.py:64
  28.0 2.6 %collective-permute-done.8 = bf16[32,512]{1,0:T(8,128)(2,1)S(1)} collective-permute-done((bf16[32,512]{1,0:T(8,128)(2,1)S(1)}, bf16[32,512]{1,0:T(8,128)(2,1)S(1)}, u32[]{:S(2)}, u32[]{:S(2)}) %collective-permute-start.8) | collective-permute-done | bytes 32800 | tf_op jit(solution)/shard_map/ppermute | solution.py:64
  30.6 1.6 %collective-permute-start.11 = (bf16[3,32,512]{2,1,0:T(8,128)(2,1)S(1)}, bf16[3,32,512]{2,1,0:T(8,128)(2,1)S(1)}, u32[]{:S(2)}, u32[]{:S(2)}) collective-permute-start(bf16[3,32,512]{2,1,0:T(8,128)(2,1)S(1)} %pad_maximum_fusion.1.rest_2_), channel_id=1, source_target_pairs={{0,1},{1,0},{2,3},{3,2},{4,5},{5,4},{6,7},{7,6},{8,9},{9,8},{10,11... | collective-permute-start | bytes 294920 | tf_op jit(solution)/shard_map/ppermute | solution.py:64
  32.2 2.0 %shard_map.80 = (f32[512,512]{1,0:T(8,128)}, f32[512,512]{1,0:T(8,128)S(1)}, bf16[512,512]{1,0:T(8,128)(2,1)S(1)}, f32[512,512]{1,0:T(8,128)S(1)}, bf16[512,512]{1,0:T(8,128)(2,1)S(1)}, /*index=5*/f32[8,128]{1,0:T(8,128)S(1)}) custom-call(f32[1]{0:T(128)S(6)} %div.3.corr_ref, f32[64,512]{1,0:T(8,128)S(1)} %pad_maximum_fusion.mine_ref, ...), custom_call_target="tpu_custom_call" | custom-call | flops 1342177280 | bytes 3145728 | tf_op jit(solution)/shard_map/pallas_call | solution.py:287
  34.2 3.0 %shard_map.81 = bf16[512,512]{1,0:T(8,128)(2,1)} custom-call(f32[512,512]{1,0:T(8,128)S(1)} %get-tuple-element.24.m0, bf16[512,512]{1,0:T(8,128)(2,1)S(1)} %get-tuple-element.25.m0b, f32[512,512]{1,0:T(8,128)S(1)} %get-tuple-element.26.m1_ref, bf16[512,512]{1,0:T(8,128)(2,1)S(1)} %get-tuple-element.27.m1b_ref, f32[8,128]{1,0:T(8,128)S(1)} %get-tuple-element.28.c_ref), custom_call_target="tpu_custom_call" | custom-call | flops 805306368 | bytes 2097152 | tf_op jit(solution)/shard_map/pallas_call | solution.py:296
  37.2 0.9 %shard_map.79 = bf16[8,32,512]{2,1,0:T(8,128)(2,1)} custom-call(s32[1,128]{1,0:T(1,128)S(1)} %get-tuple-element.16.row_ref, bf16[1,32,512]{2,1,0:T(8,128)(2,1)S(1)} %bitcast.18, bf16[1,32,512]{2,1,0:T(8,128)(2,1)S(1)} %bitcast.19, bf16[3,32,512]{2,1,0:T(8,128)(2,1)S(1)} %pad_maximum_fusion.1.rest_2_, bf16[3,32,512]{2,1,0:T(8,128)(2,1)S(1)} %collective-permute-done.11.rest_3_), custom_call_target="tpu_custom_call" | custom-call | tf_op jit(solution)/shard_map/pallas_call | solution.py:306
  (16 shorter events, 0.2 us)
Async XLA Ops:
  1.6 7.8 %collective-permute-start = (bf16[2,32,512]{2,1,0:T(8,128)(2,1)S(1)}, bf16[2,32,512]{2,1,0:T(8,128)(2,1)S(1)}, u32[]{:S(2)}, u32[]{:S(2)}) collective-permute-start(bf16[2,32,512]{2,1,0:T(8,128)(2,1)S(1)} %get-tuple-element.18), channel_id=1, source_target_pairs={{0,4},{1,5},{2,6},{3,7},{4,0},{5,1},{6,2},{7,3},{8,12},{9,13},{10,... | collective-permute-start | bytes 196616 | tf_op jit(solution)/shard_map/ppermute | solution.py:64
  5.8 6.2 %collective-permute-start.1 = (bf16[2,32,512]{2,1,0:T(8,128)(2,1)S(1)}, bf16[2,32,512]{2,1,0:T(8,128)(2,1)S(1)}, u32[]{:S(2)}, u32[]{:S(2)}) collective-permute-start(bf16[2,32,512]{2,1,0:T(8,128)(2,1)S(1)} %get-tuple-element.19), channel_id=1, source_target_pairs={{0,6},{1,7},{2,4},{3,5},{4,2},{5,3},{6,0},{7,1},{8,14},{9,15},{10,... | collective-permute-start | bytes 196616 | tf_op jit(solution)/shard_map/ppermute | solution.py:64
  7.1 5.0 %collective-permute-start.2 = (bf16[2,32,512]{2,1,0:T(8,128)(2,1)S(1)}, bf16[2,32,512]{2,1,0:T(8,128)(2,1)S(1)}, u32[]{:S(2)}, u32[]{:S(2)}) collective-permute-start(bf16[2,32,512]{2,1,0:T(8,128)(2,1)S(1)} %get-tuple-element.20), channel_id=1, source_target_pairs={{0,2},{1,3},{2,0},{3,1},{4,6},{5,7},{6,4},{7,5},{8,10},{9,11},{10,... | collective-permute-start | bytes 196616 | tf_op jit(solution)/shard_map/ppermute | solution.py:64
  12.1 7.4 %copy-start = (bf16[1,512,512]{2,1,0:T(8,128)(2,1)S(1)}, bf16[1,512,512]{2,1,0:T(8,128)(2,1)}, u32[]{:S(2)}) copy-start(bf16[1,512,512]{2,1,0:T(8,128)(2,1)} %param.9) | copy-start | bytes 1572868
  12.1 4.8 %collective-permute-start.3 = (f32[32,512]{1,0:T(8,128)S(1)}, f32[32,512]{1,0:T(8,128)S(1)}, u32[]{:S(2)}, u32[]{:S(2)}) collective-permute-start(f32[32,512]{1,0:T(8,128)S(1)} %get-tuple-element.29), channel_id=1, source_target_pairs={{0,1},{1,0},{2,3},{3,2},{4,5},{5,4},{6,7},{7,6},{8,9},{9,8},{10,11... | collective-permute-start | bytes 196616 | tf_op jit(solution)/shard_map/ppermute | solution.py:64
  13.7 5.7 %collective-permute-start.5 = (f32[32,512]{1,0:T(8,128)S(1)}, f32[32,512]{1,0:T(8,128)S(1)}, u32[]{:S(2)}, u32[]{:S(2)}) collective-permute-start(f32[32,512]{1,0:T(8,128)S(1)} %get-tuple-element.29), channel_id=1, source_target_pairs={{0,17},{1,16},{2,19},{3,18},{4,21},{5,20},{6,23},{7,22},{8,25},{9,... | collective-permute-start | bytes 196616 | tf_op jit(solution)/shard_map/ppermute | solution.py:64
  15.2 4.3 %collective-permute-start.4 = (f32[32,512]{1,0:T(8,128)S(1)}, f32[32,512]{1,0:T(8,128)S(1)}, u32[]{:S(2)}, u32[]{:S(2)}) collective-permute-start(f32[32,512]{1,0:T(8,128)S(1)} %get-tuple-element.30), channel_id=1, source_target_pairs={{0,16},{1,17},{2,18},{3,19},{4,20},{5,21},{6,22},{7,23},{8,24},{9,... | collective-permute-start | bytes 196616 | tf_op jit(solution)/shard_map/ppermute | solution.py:64
  17.0 15.2 %copy-start.1 = (f32[1,512,512]{2,1,0:T(8,128)S(1)}, f32[1,512,512]{2,1,0:T(8,128)}, u32[]{:S(2)}) copy-start(f32[1,512,512]{2,1,0:T(8,128)} %param.8) | copy-start | bytes 3145732
  19.5 1.4 %collective-permute-start.6 = (f32[64,512]{1,0:T(8,128)S(1)}, f32[64,512]{1,0:T(8,128)S(1)}, u32[]{:S(2)}, u32[]{:S(2)}) collective-permute-start(f32[64,512]{1,0:T(8,128)S(1)} %pad_maximum_fusion.mine_ref), channel_id=1, source_target_pairs={{0,8},{1,9},{2,10},{3,11},{4,12},{5,13},{6,14},{7,15},{8,0},{9,1},... | collective-permute-start | bytes 393224 | tf_op jit(solution)/shard_map/ppermute | solution.py:64
  21.2 6.8 %collective-permute-start.10 = (bf16[32,512]{1,0:T(8,128)(2,1)S(1)}, bf16[32,512]{1,0:T(8,128)(2,1)S(1)}, u32[]{:S(2)}, u32[]{:S(2)}) collective-permute-start(bf16[32,512]{1,0:T(8,128)(2,1)S(1)} %shard_map.78), channel_id=1, source_target_pairs={{0,2},{1,3},{2,0},{3,1},{4,6},{5,7},{6,4},{7,5},{8,10},{9,11},{10,... | collective-permute-start | bytes 98312 | tf_op jit(solution)/shard_map/ppermute | solution.py:64
  22.2 5.8 %collective-permute-start.9 = (bf16[32,512]{1,0:T(8,128)(2,1)S(1)}, bf16[32,512]{1,0:T(8,128)(2,1)S(1)}, u32[]{:S(2)}, u32[]{:S(2)}) collective-permute-start(bf16[32,512]{1,0:T(8,128)(2,1)S(1)} %shard_map.78), channel_id=1, source_target_pairs={{0,4},{1,5},{2,6},{3,7},{4,0},{5,1},{6,2},{7,3},{8,12},{9,13},{10,... | collective-permute-start | bytes 98312 | tf_op jit(solution)/shard_map/ppermute | solution.py:64
  24.9 5.7 %collective-permute-start.8 = (bf16[32,512]{1,0:T(8,128)(2,1)S(1)}, bf16[32,512]{1,0:T(8,128)(2,1)S(1)}, u32[]{:S(2)}, u32[]{:S(2)}) collective-permute-start(bf16[32,512]{1,0:T(8,128)(2,1)S(1)} %shard_map.78), channel_id=1, source_target_pairs={{0,6},{1,7},{2,4},{3,5},{4,2},{5,3},{6,0},{7,1},{8,14},{9,15},{10,... | collective-permute-start | bytes 98312 | tf_op jit(solution)/shard_map/ppermute | solution.py:64
  26.4 10.8 %collective-permute-start.7 = (bf16[32,512]{1,0:T(8,128)(2,1)S(1)}, bf16[32,512]{1,0:T(8,128)(2,1)S(1)}, u32[]{:S(2)}, u32[]{:S(2)}) collective-permute-start(bf16[32,512]{1,0:T(8,128)(2,1)S(1)} %shard_map.78), channel_id=1, source_target_pairs={{0,1},{1,0},{2,3},{3,2},{4,5},{5,4},{6,7},{7,6},{8,9},{9,8},{10,11... | collective-permute-start | bytes 98312 | tf_op jit(solution)/shard_map/ppermute | solution.py:64
  30.6 6.6 %collective-permute-start.11 = (bf16[3,32,512]{2,1,0:T(8,128)(2,1)S(1)}, bf16[3,32,512]{2,1,0:T(8,128)(2,1)S(1)}, u32[]{:S(2)}, u32[]{:S(2)}) collective-permute-start(bf16[3,32,512]{2,1,0:T(8,128)(2,1)S(1)} %pad_maximum_fusion.1.rest_2_), channel_id=1, source_target_pairs={{0,1},{1,0},{2,3},{3,2},{4,5},{5,4},{6,7},{7,6},{8,9},{9,8},{10,11... | collective-permute-start | bytes 294920 | tf_op jit(solution)/shard_map/ppermute | solution.py:64

commit v2 on v0

--- a/solution.py
+++ b/solution.py
@@ -42,11 +42,6 @@
 
 def farthest_first(n):
     return [k for k in range(n - 1, 0, -1)]
-
-
-def halfway_first(n):
-    middle = n // 2
-    return [k for k in range(middle, n) if k] + [k for k in range(1, middle)]
 
 
 def send(x, groups, replicas, dg, dr):
@@ -231,7 +226,7 @@
     )(stay(owner_order), stay(grad_parts[0]))
 
     partial = picked[0].astype(jnp.float32)
-    for k in halfway_first(ro):
+    for k in farthest_first(ro):
         partial = partial + hop(picked[k], dg=(0, 0), dr=(k, 0)).astype(jnp.float32)
 
     offsets = [(a, d) for a in range(go) for d in range(ri)]

time: 38.3 us -> 38.3 us (level)
  transfers between devices with their start and end apart: 12 -> 12, of which waited for: 7 -> 6; matrix products, arithmetic and copies ran while one was open for 0% -> 0% of each run, Pallas kernels for 13% -> 13%
where the time goes in v2:
time: 38.3 us; the launch traced here: 38.2 us
  starting transfers between devices  17 us (44%)
  waiting for transfers between devices  12.3 us (32%)
  Pallas kernels  7.28 us (19%)
  between operations  1.45 us (4%)
    ppermute x12, starting transfers between devices, send(): return lax.ppermute(x, ('group', 'replica'), pairs)  17 us
    ppermute x12, waiting for transfers between devices, send(): return lax.ppermute(x, ('group', 'replica'), pairs)  12.3 us
    pallas_call x1, Pallas kernels, step(): pl.pallas_call(root_kernel, out_shape=half, in_specs=[VMEM] * 5, out_spec...  3 us
    pallas_call x1, Pallas kernels, step(): pl.pallas_call(stat_kernel, out_shape=[full, full, half, full, half, jax....  2.01 us
    pallas_call x1, Pallas kernels, step(): pl.pallas_call(functools.partial(pick_kernel, replicas), out_shape=[pair]...  0.99 us
    pallas_call x1, Pallas kernels, step(): pl.pallas_call(functools.partial(place_kernel, replicas, [offsets for _,...  0.88 us
  transfers between devices with their start and end apart: 12, of which 6 were waited for; matrix products, arithmetic and copies ran while one was open for 0% of the time, Pallas kernels for 13%

profile of v2, /device:TPU:0, one launch (start us, length us, event | category | flops | bytes accessed | tf_op | source)
XLA Modules:
  0.0 38.2 jit_solution(7249171912791807399)
XLA Ops:
  0.6 1.0 %shard_map.76 = (bf16[2,32,512]{2,1,0:T(8,128)(2,1)S(1)}, bf16[2,32,512]{2,1,0:T(8,128)(2,1)S(1)}, bf16[2,32,512]{2,1,0:T(8,128)(2,1)S(1)}, bf16[2,32,512]{2,1,0:T(8,128)(2,1)S(1)}, s32[1,128]{1,0:T(1,128)S(1)}) custom-call(s32[8]{0:T(128)} %order_hbm.1, bf16[8,32,512]{2,1,0:T(8,128)(2,1)} %bitcast.21), custom_call_target="tpu_custom_call" | custom-call | tf_op jit(solution)/shard_map/pallas_call | solution.py:214
  1.6 5.1 %collective-permute-start = (bf16[2,32,512]{2,1,0:T(8,128)(2,1)S(1)}, bf16[2,32,512]{2,1,0:T(8,128)(2,1)S(1)}, u32[]{:S(2)}, u32[]{:S(2)}) collective-permute-start(bf16[2,32,512]{2,1,0:T(8,128)(2,1)S(1)} %get-tuple-element.16), channel_id=1, source_target_pairs={{0,6},{1,7},{2,4},{3,5},{4,2},{5,3},{6,0},{7,1},{8,14},{9,15},{10,... | collective-permute-start | bytes 196616 | tf_op jit(solution)/shard_map/ppermute | solution.py:59
  6.8 0.6 %collective-permute-start.2 = (bf16[2,32,512]{2,1,0:T(8,128)(2,1)S(1)}, bf16[2,32,512]{2,1,0:T(8,128)(2,1)S(1)}, u32[]{:S(2)}, u32[]{:S(2)}) collective-permute-start(bf16[2,32,512]{2,1,0:T(8,128)(2,1)S(1)} %get-tuple-element.18), channel_id=1, source_target_pairs={{0,2},{1,3},{2,0},{3,1},{4,6},{5,7},{6,4},{7,5},{8,10},{9,11},{10,... | collective-permute-start | bytes 196616 | tf_op jit(solution)/shard_map/ppermute | solution.py:59
  7.4 1.8 %collective-permute-done = bf16[2,32,512]{2,1,0:T(8,128)(2,1)S(1)} collective-permute-done((bf16[2,32,512]{2,1,0:T(8,128)(2,1)S(1)}, bf16[2,32,512]{2,1,0:T(8,128)(2,1)S(1)}, u32[]{:S(2)}, u32[]{:S(2)}) %collective-permute-start) | collective-permute-done | bytes 65568 | tf_op jit(solution)/shard_map/ppermute | solution.py:59
  9.3 3.1 %collective-permute-done.1 = bf16[2,32,512]{2,1,0:T(8,128)(2,1)S(1)} collective-permute-done((bf16[2,32,512]{2,1,0:T(8,128)(2,1)S(1)}, bf16[2,32,512]{2,1,0:T(8,128)(2,1)S(1)}, u32[]{:S(2)}, u32[]{:S(2)}) %collective-permute-start.1) | collective-permute-done | bytes 65568 | tf_op jit(solution)/shard_map/ppermute | solution.py:59
  12.4 0.0 copy-start
  12.4 0.0 copy-start.1
  12.5 1.6 %collective-permute-start.3 = (f32[32,512]{1,0:T(8,128)S(1)}, f32[32,512]{1,0:T(8,128)S(1)}, u32[]{:S(2)}, u32[]{:S(2)}) collective-permute-start(f32[32,512]{1,0:T(8,128)S(1)} %get-tuple-element.25), channel_id=1, source_target_pairs={{0,1},{1,0},{2,3},{3,2},{4,5},{5,4},{6,7},{7,6},{8,9},{9,8},{10,11... | collective-permute-start | bytes 196616 | tf_op jit(solution)/shard_map/ppermute | solution.py:59
  14.0 1.4 %collective-permute-start.5 = (f32[32,512]{1,0:T(8,128)S(1)}, f32[32,512]{1,0:T(8,128)S(1)}, u32[]{:S(2)}, u32[]{:S(2)}) collective-permute-start(f32[32,512]{1,0:T(8,128)S(1)} %get-tuple-element.25), channel_id=1, source_target_pairs={{0,17},{1,16},{2,19},{3,18},{4,21},{5,20},{6,23},{7,22},{8,25},{9,... | collective-permute-start | bytes 196616 | tf_op jit(solution)/shard_map/ppermute | solution.py:59
  15.5 0.5 %collective-permute-start.4 = (f32[32,512]{1,0:T(8,128)S(1)}, f32[32,512]{1,0:T(8,128)S(1)}, u32[]{:S(2)}, u32[]{:S(2)}) collective-permute-start(f32[32,512]{1,0:T(8,128)S(1)} %get-tuple-element.26), channel_id=1, source_target_pairs={{0,16},{1,17},{2,18},{3,19},{4,20},{5,21},{6,22},{7,23},{8,24},{9,... | collective-permute-start | bytes 196616 | tf_op jit(solution)/shard_map/ppermute | solution.py:59
  16.0 0.8 %collective-permute-done.3 = f32[32,512]{1,0:T(8,128)S(1)} collective-permute-done((f32[32,512]{1,0:T(8,128)S(1)}, f32[32,512]{1,0:T(8,128)S(1)}, u32[]{:S(2)}, u32[]{:S(2)}) %collective-permute-start.3) | collective-permute-done | bytes 65568 | tf_op jit(solution)/shard_map/ppermute | solution.py:59
  16.8 2.9 %collective-permute-done.4 = f32[32,512]{1,0:T(8,128)S(1)} collective-permute-done((f32[32,512]{1,0:T(8,128)S(1)}, f32[32,512]{1,0:T(8,128)S(1)}, u32[]{:S(2)}, u32[]{:S(2)}) %collective-permute-start.4) | collective-permute-done | bytes 65568 | tf_op jit(solution)/shard_map/ppermute | solution.py:59
  19.8 0.1 collective-permute-start.6
  19.9 1.3 %collective-permute-done.6.other_ref = f32[64,512]{1,0:T(8,128)S(1)} collective-permute-done((f32[64,512]{1,0:T(8,128)S(1)}, f32[64,512]{1,0:T(8,128)S(1)}, u32[]{:S(2)}, u32[]{:S(2)}) %collective-permute-start.6) | collective-permute-done | bytes 131104 | tf_op jit(solution)/shard_map/ppermute | solution.py:59
  21.2 0.4 %shard_map.77 = bf16[32,512]{1,0:T(8,128)(2,1)S(1)} custom-call(f32[64,512]{1,0:T(8,128)S(1)} %pad_maximum_fusion.mine_ref, f32[64,512]{1,0:T(8,128)S(1)} %collective-permute-done.6.other_ref, bf16[512,512]{1,0:T(8,128)(2,1)S(1)} %bitcast.16), custom_call_target="tpu_custom_call" | custom-call | flops 67108864 | bytes 262144 | tf_op jit(solution)/shard_map/pallas_call | solution.py:240
  21.6 1.1 %collective-permute-start.10 = (bf16[32,512]{1,0:T(8,128)(2,1)S(1)}, bf16[32,512]{1,0:T(8,128)(2,1)S(1)}, u32[]{:S(2)}, u32[]{:S(2)}) collective-permute-start(bf16[32,512]{1,0:T(8,128)(2,1)S(1)} %shard_map.77), channel_id=1, source_target_pairs={{0,2},{1,3},{2,0},{3,1},{4,6},{5,7},{6,4},{7,5},{8,10},{9,11},{10,... | collective-permute-start | bytes 98312 | tf_op jit(solution)/shard_map/ppermute | solution.py:59
  22.8 2.2 %collective-permute-start.9 = (bf16[32,512]{1,0:T(8,128)(2,1)S(1)}, bf16[32,512]{1,0:T(8,128)(2,1)S(1)}, u32[]{:S(2)}, u32[]{:S(2)}) collective-permute-start(bf16[32,512]{1,0:T(8,128)(2,1)S(1)} %shard_map.77), channel_id=1, source_target_pairs={{0,4},{1,5},{2,6},{3,7},{4,0},{5,1},{6,2},{7,3},{8,12},{9,13},{10,... | collective-permute-start | bytes 98312 | tf_op jit(solution)/shard_map/ppermute | solution.py:59
  25.0 1.1 %collective-permute-start.8 = (bf16[32,512]{1,0:T(8,128)(2,1)S(1)}, bf16[32,512]{1,0:T(8,128)(2,1)S(1)}, u32[]{:S(2)}, u32[]{:S(2)}) collective-permute-start(bf16[32,512]{1,0:T(8,128)(2,1)S(1)} %shard_map.77), channel_id=1, source_target_pairs={{0,6},{1,7},{2,4},{3,5},{4,2},{5,3},{6,0},{7,1},{8,14},{9,15},{10,... | collective-permute-start | bytes 98312 | tf_op jit(solution)/shard_map/ppermute | solution.py:59
  26.8 1.6 %collective-permute-start.7 = (bf16[32,512]{1,0:T(8,128)(2,1)S(1)}, bf16[32,512]{1,0:T(8,128)(2,1)S(1)}, u32[]{:S(2)}, u32[]{:S(2)}) collective-permute-start(bf16[32,512]{1,0:T(8,128)(2,1)S(1)} %shard_map.77), channel_id=1, source_target_pairs={{0,1},{1,0},{2,3},{3,2},{4,5},{5,4},{6,7},{7,6},{8,9},{9,8},{10,11... | collective-permute-start | bytes 98312 | tf_op jit(solution)/shard_map/ppermute | solution.py:59
  28.4 2.3 %collective-permute-done.8 = bf16[32,512]{1,0:T(8,128)(2,1)S(1)} collective-permute-done((bf16[32,512]{1,0:T(8,128)(2,1)S(1)}, bf16[32,512]{1,0:T(8,128)(2,1)S(1)}, u32[]{:S(2)}, u32[]{:S(2)}) %collective-permute-start.8) | collective-permute-done | bytes 32800 | tf_op jit(solution)/shard_map/ppermute | solution.py:59
  30.7 1.6 %collective-permute-start.11 = (bf16[3,32,512]{2,1,0:T(8,128)(2,1)S(1)}, bf16[3,32,512]{2,1,0:T(8,128)(2,1)S(1)}, u32[]{:S(2)}, u32[]{:S(2)}) collective-permute-start(bf16[3,32,512]{2,1,0:T(8,128)(2,1)S(1)} %pad_maximum_fusion.1.rest_2_), channel_id=1, source_target_pairs={{0,1},{1,0},{2,3},{3,2},{4,5},{5,4},{6,7},{7,6},{8,9},{9,8},{10,11... | collective-permute-start | bytes 294920 | tf_op jit(solution)/shard_map/ppermute | solution.py:59
  32.3 2.0 %shard_map.79 = (f32[512,512]{1,0:T(8,128)}, f32[512,512]{1,0:T(8,128)S(1)}, bf16[512,512]{1,0:T(8,128)(2,1)S(1)}, f32[512,512]{1,0:T(8,128)S(1)}, bf16[512,512]{1,0:T(8,128)(2,1)S(1)}, /*index=5*/f32[8,128]{1,0:T(8,128)S(1)}) custom-call(f32[1]{0:T(128)S(6)} %div.3.corr_ref, f32[64,512]{1,0:T(8,128)S(1)} %pad_maximum_fusion.mine_ref, ...), custom_call_target="tpu_custom_call" | custom-call | flops 1342177280 | bytes 3145728 | tf_op jit(solution)/shard_map/pallas_call | solution.py:264
  34.3 3.0 %shard_map.80 = bf16[512,512]{1,0:T(8,128)(2,1)} custom-call(f32[512,512]{1,0:T(8,128)S(1)} %get-tuple-element.20.m0, bf16[512,512]{1,0:T(8,128)(2,1)S(1)} %get-tuple-element.21.m0b, f32[512,512]{1,0:T(8,128)S(1)} %get-tuple-element.22.m1_ref, bf16[512,512]{1,0:T(8,128)(2,1)S(1)} %get-tuple-element.23.m1b_ref, f32[8,128]{1,0:T(8,128)S(1)} %get-tuple-element.24.c_ref), custom_call_target="tpu_custom_call" | custom-call | flops 805306368 | bytes 2097152 | tf_op jit(solution)/shard_map/pallas_call | solution.py:273
  37.3 0.9 %shard_map.78 = bf16[8,32,512]{2,1,0:T(8,128)(2,1)} custom-call(s32[1,128]{1,0:T(1,128)S(1)} %get-tuple-element.14.row_ref, bf16[1,32,512]{2,1,0:T(8,128)(2,1)S(1)} %bitcast.17, bf16[1,32,512]{2,1,0:T(8,128)(2,1)S(1)} %bitcast.18, bf16[3,32,512]{2,1,0:T(8,128)(2,1)S(1)} %pad_maximum_fusion.1.rest_2_, bf16[3,32,512]{2,1,0:T(8,128)(2,1)S(1)} %collective-permute-done.11.rest_3_), custom_call_target="tpu_custom_call" | custom-call | tf_op jit(solution)/shard_map/pallas_call | solution.py:283
  (15 shorter events, 0.1 us)
Async XLA Ops:
  1.6 7.6 %collective-permute-start = (bf16[2,32,512]{2,1,0:T(8,128)(2,1)S(1)}, bf16[2,32,512]{2,1,0:T(8,128)(2,1)S(1)}, u32[]{:S(2)}, u32[]{:S(2)}) collective-permute-start(bf16[2,32,512]{2,1,0:T(8,128)(2,1)S(1)} %get-tuple-element.16), channel_id=1, source_target_pairs={{0,6},{1,7},{2,4},{3,5},{4,2},{5,3},{6,0},{7,1},{8,14},{9,15},{10,... | collective-permute-start | bytes 196616 | tf_op jit(solution)/shard_map/ppermute | solution.py:59
  6.8 5.6 %collective-permute-start.1 = (bf16[2,32,512]{2,1,0:T(8,128)(2,1)S(1)}, bf16[2,32,512]{2,1,0:T(8,128)(2,1)S(1)}, u32[]{:S(2)}, u32[]{:S(2)}) collective-permute-start(bf16[2,32,512]{2,1,0:T(8,128)(2,1)S(1)} %get-tuple-element.17), channel_id=1, source_target_pairs={{0,4},{1,5},{2,6},{3,7},{4,0},{5,1},{6,2},{7,3},{8,12},{9,13},{10,... | collective-permute-start | bytes 196616 | tf_op jit(solution)/shard_map/ppermute | solution.py:59
  6.8 5.6 %collective-permute-start.2 = (bf16[2,32,512]{2,1,0:T(8,128)(2,1)S(1)}, bf16[2,32,512]{2,1,0:T(8,128)(2,1)S(1)}, u32[]{:S(2)}, u32[]{:S(2)}) collective-permute-start(bf16[2,32,512]{2,1,0:T(8,128)(2,1)S(1)} %get-tuple-element.18), channel_id=1, source_target_pairs={{0,2},{1,3},{2,0},{3,1},{4,6},{5,7},{6,4},{7,5},{8,10},{9,11},{10,... | collective-permute-start | bytes 196616 | tf_op jit(solution)/shard_map/ppermute | solution.py:59
  12.4 8.8 %copy-start = (bf16[1,512,512]{2,1,0:T(8,128)(2,1)S(1)}, bf16[1,512,512]{2,1,0:T(8,128)(2,1)}, u32[]{:S(2)}) copy-start(bf16[1,512,512]{2,1,0:T(8,128)(2,1)} %param.9) | copy-start | bytes 1572868
  12.4 19.8 %copy-start.1 = (f32[1,512,512]{2,1,0:T(8,128)S(1)}, f32[1,512,512]{2,1,0:T(8,128)}, u32[]{:S(2)}) copy-start(f32[1,512,512]{2,1,0:T(8,128)} %param.8) | copy-start | bytes 3145732
  12.5 4.3 %collective-permute-start.3 = (f32[32,512]{1,0:T(8,128)S(1)}, f32[32,512]{1,0:T(8,128)S(1)}, u32[]{:S(2)}, u32[]{:S(2)}) collective-permute-start(f32[32,512]{1,0:T(8,128)S(1)} %get-tuple-element.25), channel_id=1, source_target_pairs={{0,1},{1,0},{2,3},{3,2},{4,5},{5,4},{6,7},{7,6},{8,9},{9,8},{10,11... | collective-permute-start | bytes 196616 | tf_op jit(solution)/shard_map/ppermute | solution.py:59
  14.0 5.7 %collective-permute-start.5 = (f32[32,512]{1,0:T(8,128)S(1)}, f32[32,512]{1,0:T(8,128)S(1)}, u32[]{:S(2)}, u32[]{:S(2)}) collective-permute-start(f32[32,512]{1,0:T(8,128)S(1)} %get-tuple-element.25), channel_id=1, source_target_pairs={{0,17},{1,16},{2,19},{3,18},{4,21},{5,20},{6,23},{7,22},{8,25},{9,... | collective-permute-start | bytes 196616 | tf_op jit(solution)/shard_map/ppermute | solution.py:59
  15.5 4.3 %collective-permute-start.4 = (f32[32,512]{1,0:T(8,128)S(1)}, f32[32,512]{1,0:T(8,128)S(1)}, u32[]{:S(2)}, u32[]{:S(2)}) collective-permute-start(f32[32,512]{1,0:T(8,128)S(1)} %get-tuple-element.26), channel_id=1, source_target_pairs={{0,16},{1,17},{2,18},{3,19},{4,20},{5,21},{6,22},{7,23},{8,24},{9,... | collective-permute-start | bytes 196616 | tf_op jit(solution)/shard_map/ppermute | solution.py:59
  19.8 1.4 %collective-permute-start.6 = (f32[64,512]{1,0:T(8,128)S(1)}, f32[64,512]{1,0:T(8,128)S(1)}, u32[]{:S(2)}, u32[]{:S(2)}) collective-permute-start(f32[64,512]{1,0:T(8,128)S(1)} %pad_maximum_fusion.mine_ref), channel_id=1, source_target_pairs={{0,8},{1,9},{2,10},{3,11},{4,12},{5,13},{6,14},{7,15},{8,0},{9,1},... | collective-permute-start | bytes 393224 | tf_op jit(solution)/shard_map/ppermute | solution.py:59
  21.6 6.8 %collective-permute-start.10 = (bf16[32,512]{1,0:T(8,128)(2,1)S(1)}, bf16[32,512]{1,0:T(8,128)(2,1)S(1)}, u32[]{:S(2)}, u32[]{:S(2)}) collective-permute-start(bf16[32,512]{1,0:T(8,128)(2,1)S(1)} %shard_map.77), channel_id=1, source_target_pairs={{0,2},{1,3},{2,0},{3,1},{4,6},{5,7},{6,4},{7,5},{8,10},{9,11},{10,... | collective-permute-start | bytes 98312 | tf_op jit(solution)/shard_map/ppermute | solution.py:59
  22.8 5.6 %collective-permute-start.9 = (bf16[32,512]{1,0:T(8,128)(2,1)S(1)}, bf16[32,512]{1,0:T(8,128)(2,1)S(1)}, u32[]{:S(2)}, u32[]{:S(2)}) collective-permute-start(bf16[32,512]{1,0:T(8,128)(2,1)S(1)} %shard_map.77), channel_id=1, source_target_pairs={{0,4},{1,5},{2,6},{3,7},{4,0},{5,1},{6,2},{7,3},{8,12},{9,13},{10,... | collective-permute-start | bytes 98312 | tf_op jit(solution)/shard_map/ppermute | solution.py:59
  25.0 5.7 %collective-permute-start.8 = (bf16[32,512]{1,0:T(8,128)(2,1)S(1)}, bf16[32,512]{1,0:T(8,128)(2,1)S(1)}, u32[]{:S(2)}, u32[]{:S(2)}) collective-permute-start(bf16[32,512]{1,0:T(8,128)(2,1)S(1)} %shard_map.77), channel_id=1, source_target_pairs={{0,6},{1,7},{2,4},{3,5},{4,2},{5,3},{6,0},{7,1},{8,14},{9,15},{10,... | collective-permute-start | bytes 98312 | tf_op jit(solution)/shard_map/ppermute | solution.py:59
  26.8 10.5 %collective-permute-start.7 = (bf16[32,512]{1,0:T(8,128)(2,1)S(1)}, bf16[32,512]{1,0:T(8,128)(2,1)S(1)}, u32[]{:S(2)}, u32[]{:S(2)}) collective-permute-start(bf16[32,512]{1,0:T(8,128)(2,1)S(1)} %shard_map.77), channel_id=1, source_target_pairs={{0,1},{1,0},{2,3},{3,2},{4,5},{5,4},{6,7},{7,6},{8,9},{9,8},{10,11... | collective-permute-start | bytes 98312 | tf_op jit(solution)/shard_map/ppermute | solution.py:59
  30.7 6.6 %collective-permute-start.11 = (bf16[3,32,512]{2,1,0:T(8,128)(2,1)S(1)}, bf16[3,32,512]{2,1,0:T(8,128)(2,1)S(1)}, u32[]{:S(2)}, u32[]{:S(2)}) collective-permute-start(bf16[3,32,512]{2,1,0:T(8,128)(2,1)S(1)} %pad_maximum_fusion.1.rest_2_), channel_id=1, source_target_pairs={{0,1},{1,0},{2,3},{3,2},{4,5},{5,4},{6,7},{7,6},{8,9},{9,8},{10,11... | collective-permute-start | bytes 294920 | tf_op jit(solution)/shard_map/ppermute | solution.py:59
